TPU v7x, 32 devices: a whole 2x2x4 slice. The times are simulated.
32 devices in a mesh: gx: 8 (over y, x, core), gy: 4 (over z).
Axes of the slice: x: 2, y: 2, z: 4, core: 2. Of those that a mesh axis runs over, the one named last changes fastest.
Arguments:
- distribution: float32 [8, 32, 32768], P('gx', 'gy'), may hold values from 0.2 to 2
- relax_rate: float32 [8, 32], P('gx', 'gy'), may hold values from 0.05 to 0.8
- block_level: int32 [8], replicated, may hold values from 0 to 1, as said below
- block_link: int32 [2, 64], replicated, may hold values from 0 to 7, as said below
- remap_values: bfloat16 [2, 64, 512, 512], P(None, 'gy'), may hold values from -0.25 to 0.25
Outputs:
- updated: float32 [8, 32, 32768], P('gx', 'gy')
Inputs may be any that keep to these rules, and one draw needn't show every extreme that they name: `block_level`: every maximal run of streamwise blocks with one level holds at least two blocks; the first run holds exactly two, so the level changes between blocks 1 and 2. `block_link`: in each direction every coarse block is named by exactly 8 fine blocks.
All inputs are finite; a program needn't handle non-finite values.
Results may differ from a plain program's by a relative error of at most 0.00095.
Values may be sent and summed in bfloat16 or wider, within the bound.
No kernel may reach another device: no remote copies, remote signals or barrier semaphores. Data moves between devices by JAX's collectives and lax.ppermute only.
A program may use at most 64 MiB of HBM per device.

v0:
```python
import functools
import math

import jax
import jax.numpy as jnp
from jax import lax
from jax.experimental import pallas as pl
from jax.experimental.pallas import tpu as pltpu
from jax.sharding import PartitionSpec as P

SC = 16
SF = 32
BLK = 512
NVC = 4096
NVF = 32768
VBC = NVC // BLK
VBF = NVF // BLK
HALF_F = VBF // 2
HALF_C = VBC // 2
CHUNKS = 8
PART = NVF // CHUNKS

cfl_ratio = 0.03
spacing_coarse = 0.5
spacing_fine = 0.4

BOTH = ("gx", "gy")
SMEM = pl.BlockSpec(memory_space=pltpu.SMEM)
VMEM = pl.BlockSpec(memory_space=pltpu.VMEM)
HBM = pl.BlockSpec(memory_space=pltpu.HBM)
F32 = jnp.float32
BF16 = jnp.bfloat16


def place(level_ref):
    block = lax.axis_index("gx")
    own = level_ref[block]
    lower = level_ref[jnp.maximum(block - 1, 0)]
    upper = level_ref[jnp.minimum(block + 1, level_ref.shape[0] - 1)]
    return block, own, lower != own, upper != own


def peer(me, step, group):
    if group & (group - 1):
        raise ValueError(group)
    return me ^ step


def order(group):
    return sorted(range(group), key=lambda s: (s == 1, s))


def entry(group):
    return sorted(range(group), key=lambda s: (s > 0, s == group - 1, s != group // 2, s))


def near(group):
    return [s for s in entry(group) if s and not s & (s + 1)]


def sizes(local):
    return [max(1, (5 * local) // 8), max(1, (3 * local) // 4), local]


def block_at(ref, index):
    return ref[:, pl.ds(pl.multiple_of(index * BLK, BLK), BLK)]


def prepare_kernel(level_ref, link_ref, cells_ref, even_ref, odd_ref, index_ref):
    block, own, lower_differs, upper_differs = place(level_ref)
    fine = own == 1

    def fill(target_ref, going_up):
        differs = jnp.where(going_up, upper_differs, lower_differs)
        gathers = differs & fine

        @pl.when(gathers)
        def _():
            def look(f, count):
                index_ref[count] = f
                hit = (link_ref[1, f] >= HALF_C) == going_up
                return count + hit.astype(jnp.int32)

            lax.fori_loop(0, VBF, look, jnp.int32(0), unroll=8)

            def copy(j, carry):
                target_ref[j] = block_at(cells_ref, index_ref[j]).astype(BF16)
                return carry

            lax.fori_loop(0, HALF_F, copy, 0, unroll=8)

        @pl.when(fine & jnp.logical_not(differs))
        def _():
            start = jnp.where(going_up, HALF_F, 0)
            for j in range(HALF_F):
                target_ref[j] = block_at(cells_ref, start + j).astype(BF16)

        @pl.when(jnp.logical_not(fine))
        def _():
            start = jnp.where(going_up & jnp.logical_not(differs), HALF_C, 0)
            for j in range(VBC):
                target_ref[j] = block_at(cells_ref, start + j).astype(BF16)

    on_even = block % 2 == 0
    fill(odd_ref, jnp.logical_not(on_even))
    fill(even_ref, on_even)


def prepare(levels, links, cells):
    half = jax.ShapeDtypeStruct((HALF_F, cells.shape[0], BLK), BF16)
    return pl.pallas_call(
        prepare_kernel,
        name="prepare",
        out_shape=(half, half),
        in_specs=[SMEM, SMEM, VMEM],
        out_specs=(VMEM,) * 2,
        scratch_shapes=[pltpu.SMEM((VBF + 1,), jnp.int32)],
        cost_estimate=pl.CostEstimate(flops=10**6, bytes_accessed=2 * 10**6, transcendentals=0),
        compiler_params=pltpu.CompilerParams(vmem_limit_bytes=8 << 20),
    )(levels, links, cells)


def rows_kernel(level_ref, cells_ref, ahead_ref, back_ref, row_ref):
    _, own, _, _ = place(level_ref)
    cells_y = cells_ref.shape[0]

    def rows(target_ref, row, parity):
        @pl.when(own == 1)
        def _():
            for i in range(HALF_F):
                row_ref[i : i + 1, :] = cells_ref[
                    row : row + 1, (2 * i + parity) * BLK : (2 * i + parity + 1) * BLK
                ]

        @pl.when(own != 1)
        def _():
            for i in range(VBC):
                row_ref[i : i + 1, :] = cells_ref[row : row + 1, i * BLK : (i + 1) * BLK]

        target_ref[...] = row_ref[...].astype(BF16)

    rows(ahead_ref, cells_y - 1, 1)
    rows(back_ref, 0, 0)


def edge_rows(levels, cells):
    row = jax.ShapeDtypeStruct((HALF_F, BLK), BF16)
    return pl.pallas_call(
        rows_kernel,
        name="edge_rows",
        out_shape=(row, row),
        in_specs=[SMEM, VMEM],
        out_specs=(VMEM, VMEM),
        scratch_shapes=[pltpu.VMEM((HALF_F, BLK), F32)],
        cost_estimate=pl.CostEstimate(flops=10**6, bytes_accessed=2 * 10**6, transcendentals=0),
        compiler_params=pltpu.CompilerParams(vmem_limit_bytes=8 << 20),
    )(levels, cells)


def ghost_at(ref, index):
    return ref[index].astype(F32)


def relax_kernel(
    level,
    level_ref,
    rate_ref,
    cells_ref,
    even_ref,
    odd_ref,
    *refs,
):
    side_ref, done_ref, sems = refs[-3:]
    results = 1 if level is None else 2
    row_refs, out_ref = refs[: -3 - results], refs[-3 - results]
    block, own, lower_differs, upper_differs = place(level_ref)
    on_even = block % 2 == 0
    rows_n = cells_ref.shape[0]

    def flush(chunk):
        at = pl.ds(chunk * PART, PART)
        return pltpu.make_async_copy(done_ref.at[:, at], out_ref.at[:, at], sems.at[chunk])

    def run(side, spacing):
        width = side * side
        mid = width // 2
        middle = side // 2
        centre = (side - 1) * 0.5
        lane = lax.broadcasted_iota(jnp.int32, (rows_n, width), 1)
        along_y = spacing * ((lane // side).astype(F32) - centre)
        along_z = spacing * ((lane % side).astype(F32) - centre)

        def span(i):
            start = i * width
            return pl.ds(start if isinstance(i, int) else pl.multiple_of(start, width), width)

        def speed_at(i):
            return spacing * (lax.convert_element_type(i, F32) - centre)

        def gather(i, sums):
            total, first, second = sums
            plane = cells_ref[:, span(i)]
            speed = speed_at(i)
            return total + plane, first + plane * speed, second + plane * (speed * speed)

        zero = jnp.zeros((rows_n, width), F32)
        total, first, second = lax.fori_loop(0, side, gather, (zero, zero, zero), unroll=4)

        def over(value):
            return jnp.broadcast_to(jnp.sum(value, axis=1, keepdims=True), (rows_n, 128))

        weight = spacing * spacing * spacing
        density = weight * over(total)
        scale = weight / density
        mean_x = scale * over(first)
        mean_y = scale * over(total * along_y)
        mean_z = scale * over(total * along_z)
        square = scale * over(second + total * (along_y * along_y + along_z * along_z))
        heat = (square - mean_x * mean_x - mean_y * mean_y - mean_z * mean_z) / 3.0
        row = lax.broadcasted_iota(jnp.int32, (rows_n, 128), 0)
        rate = jnp.zeros((rows_n, 128), F32)
        for r in range(rows_n):
            rate = jnp.where(row == r, rate_ref[0, r], rate)
        spread = 2.0 * math.pi * heat
        peak = rate * density / (spread * jnp.sqrt(spread))
        inverse = -0.5 / heat

        def wide(value):
            return jnp.concatenate([value] * (width // 128), axis=1)

        off_y = along_y - wide(mean_y)
        off_z = along_z - wide(mean_z)
        across = wide(peak) * jnp.exp((off_y * off_y + off_z * off_z) * wide(inverse))
        drift = cfl_ratio * jnp.abs(along_y)
        keep = (1.0 - wide(rate)) - drift
        wide_row = lax.broadcasted_iota(jnp.int32, (rows_n, mid), 0)

        def update(i, upward):
            plane = cells_ref[:, span(i)]
            speed = speed_at(i)
            off_x = speed - mean_x
            along = wide(jnp.exp(off_x * off_x * inverse))
            take_even = on_even == upward
            if side == SF:
                right = side_ref[1, pl.ds(i, 1), :]
                left = side_ref[0, pl.ds(i, 1), :]
                slot = 2 * (i if upward else i - middle)
                ghosts = []
                for half in range(2):
                    a, b = ghost_at(even_ref, slot + half), ghost_at(odd_ref, slot + half)
                    ghosts.append(jnp.where(take_even, a, b))
                ghost = jnp.concatenate(ghosts, axis=1)
            else:
                slot, offset = i // 2, (i % 2) * width
                right = side_ref[1, slot : slot + 1, offset : offset + mid]
                left = side_ref[0, slot : slot + 1, offset + mid : offset + width]
                slot = slot if upward else slot - HALF_C
                a, b = ghost_at(even_ref, slot), ghost_at(odd_ref, slot)
                ghost = jnp.where(take_even, a, b)[:, offset : offset + width]
            if level is not None:
                ghost = jnp.where(upper_differs if upward else lower_differs, 0.0, ghost)
            low, high = plane[:, :mid], plane[:, mid:]
            beyond = jnp.where(wide_row == rows_n - 1, right, pltpu.roll(low, rows_n - 1, 0))
            before = jnp.where(wide_row == 0, left, pltpu.roll(high, 1, 0))
            beside = jnp.concatenate([beyond, before], axis=1)
            push = cfl_ratio * jnp.abs(speed)
            done_ref[:, span(i)] = (
                plane * (keep - push) + push * ghost + drift * beside + along * across
            )

        if side == SF:
            each = side // CHUNKS
            for chunk in range(CHUNKS):
                upward = chunk < CHUNKS // 2

                def step(k, carry, chunk=chunk, upward=upward):
                    update(chunk * each + k, upward)
                    return carry

                lax.fori_loop(0, each, step, 0, unroll=4)
                flush(chunk).start()
        else:
            for i in range(side):
                update(i, i < middle)
            flush(0).start()
            done_ref[:, NVC:] = jnp.zeros((rows_n, NVF - NVC), F32)
            for chunk in range(1, CHUNKS):
                flush(chunk).start()

    if level is None:
        for k, row_ref in enumerate(row_refs):
            side_ref[k] = row_ref[...].astype(F32)
    else:
        side_ref[...] = jnp.zeros_like(side_ref)
        me, group = lax.axis_index("gy"), lax.axis_size("gy")
        for s, ref in zip(entry(group)[1:], row_refs):
            if s not in near(group):
                continue
            first = ref.shape[0] - ROWS
            for k, by in ((0, -1), (1, 1)):

                @pl.when(peer(me, s, group) == me + by)
                def _(ref=ref, k=k, first=first):
                    for j in range(ROWS):
                        side_ref[k, 8 * j : 8 * j + 8, :] = ref[first + j].astype(F32)

    if level is None:

        @pl.when(own == 1)
        def _():
            run(SF, spacing_fine)

        @pl.when(own != 1)
        def _():
            run(SC, spacing_coarse)

    elif level == 1:
        run(SF, spacing_fine)
    else:
        run(SC, spacing_coarse)

    if level is not None:
        base_ref = refs[-4]
        split = (NVF if level == 1 else NVC) // 2

        @pl.when(upper_differs)
        def _():
            base_ref[...] = done_ref[:, :split]

        @pl.when(jnp.logical_not(upper_differs))
        def _():
            base_ref[...] = done_ref[:, split : 2 * split]

    for chunk in range(CHUNKS):
        flush(chunk).wait()


def relax(level, levels, rate, cells, even, odd, rows):
    out = jax.ShapeDtypeStruct(cells.shape, F32)
    half = jax.ShapeDtypeStruct((cells.shape[0], (NVF if level == 1 else NVC) // 2), F32)
    return pl.pallas_call(
        functools.partial(relax_kernel, level),
        name="relax",
        out_shape=(out,) if level is None else (out, half),
        in_specs=[SMEM, SMEM, VMEM, VMEM, VMEM] + [VMEM] * len(rows),
        out_specs=(HBM,) if level is None else (HBM, VMEM),
        scratch_shapes=[
            pltpu.VMEM((2, HALF_F, BLK), F32),
            pltpu.VMEM(cells.shape, F32),
            pltpu.SemaphoreType.DMA((CHUNKS,)),
        ],
        cost_estimate=pl.CostEstimate(flops=10**7, bytes_accessed=4 * 10**6, transcendentals=10**5),
        compiler_params=pltpu.CompilerParams(vmem_limit_bytes=16 << 20),
    )(levels, rate, cells, even, odd, *rows)


ROWS = HALF_F // 8


def attach(group, ahead_ref, back_ref, out_refs):
    me = lax.axis_index("gy")
    for s, out_ref in zip(entry(group), out_refs):
        if s not in near(group):
            continue
        first = out_ref.shape[0] - ROWS
        for source_ref, by in ((ahead_ref, 1), (back_ref, -1)):

            @pl.when(peer(me, s, group) == me + by)
            def _(out_ref=out_ref, source_ref=source_ref, first=first):
                for j in range(ROWS):
                    out_ref[first + j] = source_ref[8 * j : 8 * j + 8, :]


def coarse_kernel(group, level_ref, even_ref, odd_ref, ahead_ref, back_ref, *out_refs):
    block, _, lower_differs, _ = place(level_ref)
    use_even = (block % 2 == 0) != lower_differs
    for j in range(VBC):
        a, b = even_ref[j].astype(F32), odd_ref[j].astype(F32)
        piece = jnp.where(use_even, a, b).astype(BF16)
        for out_ref in out_refs:
            out_ref[j] = piece
    attach(group, ahead_ref, back_ref, out_refs)


def pieces_kernel(group, level_ref, link_ref, even_ref, odd_ref, ahead_ref, back_ref, *refs):
    out_refs, start_ref = refs[:-1], refs[-1]
    block, own, lower_differs, _ = place(level_ref)
    me = lax.axis_index("gy")
    local = VBF // group
    slots = out_refs[0].shape[0]
    use_even = (block % 2 == 0) != lower_differs

    def count(h, total):
        start_ref[h] = total
        for j in range(local):
            hit = (link_ref[1, h * local + j] >= HALF_C) == lower_differs
            total = total + hit.astype(jnp.int32)
        return total

    lax.fori_loop(0, group, count, jnp.int32(0))

    def fill(source_ref):
        for s, out_ref in zip(entry(group), out_refs):
            start = start_ref[peer(me, s, group)]
            for j in range(slots):
                out_ref[j] = source_ref[jnp.minimum(start + j, HALF_F - 1)]

    @pl.when(use_even)
    def _():
        fill(even_ref)

    @pl.when(jnp.logical_not(use_even))
    def _():
        fill(odd_ref)

    attach(group, ahead_ref, back_ref, out_refs)


def outgoing_shapes(slots, group, rows_n):
    return tuple(
        jax.ShapeDtypeStruct((slots + (ROWS if s else 0), rows_n, BLK), BF16)
        for s in entry(group)
    )


def coarse_pieces(levels, even, odd, edges, group):
    return pl.pallas_call(
        functools.partial(coarse_kernel, group),
        name="coarse_pieces",
        out_shape=outgoing_shapes(VBC, group, even.shape[1]),
        in_specs=[SMEM] + [VMEM] * 4,
        out_specs=(VMEM,) * group,
        cost_estimate=pl.CostEstimate(flops=10**5, bytes_accessed=10**6, transcendentals=0),
        compiler_params=pltpu.CompilerParams(vmem_limit_bytes=8 << 20),
    )(levels, even, odd, *edges)


def pieces(levels, links, even, odd, edges, group, slots):
    return pl.pallas_call(
        functools.partial(pieces_kernel, group),
        name="pieces",
        out_shape=outgoing_shapes(slots, group, even.shape[1]),
        in_specs=[SMEM, SMEM] + [VMEM] * 4,
        out_specs=(VMEM,) * group,
        scratch_shapes=[pltpu.SMEM((group,), jnp.int32)],
        cost_estimate=pl.CostEstimate(flops=10**5, bytes_accessed=10**6, transcendentals=0),
        compiler_params=pltpu.CompilerParams(vmem_limit_bytes=8 << 20),
    )(levels, links, even, odd, *edges)


def stacked(refs, index):
    return jnp.concatenate([ref[index].astype(F32) for ref in refs], axis=0).astype(BF16)


def to_coarse_kernel(group, level_ref, link_ref, values_ref, *refs):
    in_refs, out_refs, sum_ref = refs[:group], refs[group : 2 * group], refs[-1]
    _, _, lower_differs, _ = place(level_ref)
    local = values_ref.shape[0]
    cells_y = in_refs[0].shape[1]
    first = lax.axis_index("gy") * local
    offset = jnp.where(lower_differs, HALF_C, 0)

    targets = [link_ref[1, first + j] - offset for j in range(local)]
    needed = [(t >= 0) & (t < HALF_C) for t in targets]
    sum_ref[...] = jnp.zeros_like(sum_ref)
    slot = jnp.int32(0)
    for j in range(local):

        @pl.when(needed[j])
        def _(j=j, slot=slot):
            sum_ref[targets[j]] += jnp.dot(
                stacked(in_refs, slot), values_ref[j], preferred_element_type=F32
            )

        slot = slot + needed[j].astype(jnp.int32)
    for s, out_ref in enumerate(out_refs):
        out_ref[...] = sum_ref[:, s * cells_y : (s + 1) * cells_y, :].astype(BF16)


def to_fine_kernel(group, level_ref, link_ref, values_ref, *refs):
    in_refs, out_refs = refs[:group], refs[group : 2 * group]
    _, _, lower_differs, _ = place(level_ref)
    local = values_ref.shape[0]
    cells_y = in_refs[0].shape[1]
    first = lax.axis_index("gy") * local
    active = (first >= HALF_F) == lower_differs

    @pl.when(active)
    def _():
        for j in range(local):
            product = jnp.dot(
                stacked(in_refs, link_ref[0, first + j]),
                values_ref[j],
                preferred_element_type=F32,
            ).astype(BF16)
            for s, out_ref in enumerate(out_refs):
                out_ref[j] = product[s * cells_y : (s + 1) * cells_y, :]


def load_kernel(level_ref, link_ref, values_ref, role_ref, held_ref, sems):
    _, own, lower_differs, upper_differs = place(level_ref)
    local = values_ref.shape[1]
    first = lax.axis_index("gy") * local
    fine = own == 1
    differs = lower_differs | upper_differs
    counts = sizes(local)
    fine_role = len(counts) + jnp.where(lower_differs, 1, 2)
    role_ref[0] = jnp.where(differs & fine, fine_role, 0)

    @pl.when(differs & fine & ((first >= HALF_F) == lower_differs))
    def _():
        whole = pltpu.make_async_copy(values_ref.at[0], held_ref, sems.at[0])
        whole.start()
        whole.wait()

    @pl.when(differs & jnp.logical_not(fine))
    def _():
        def hit(f):
            return (link_ref[1, f] >= HALF_C) == lower_differs

        def copy(j):
            return pltpu.make_async_copy(values_ref.at[1, j], held_ref.at[j], sems.at[j])

        needed = [hit(first + j) for j in range(local)]
        for j in range(local):
            pl.when(needed[j])(lambda j=j: copy(j).start())

        def most(h, worst):
            count = jnp.int32(0)
            for j in range(local):
                count = count + hit(h * local + j).astype(jnp.int32)
            return jnp.maximum(worst, count)

        worst = lax.fori_loop(0, VBF // local, most, jnp.int32(0))
        role = jnp.int32(1)
        for size in counts[:-1]:
            role = role + (worst > size).astype(jnp.int32)
        role_ref[0] = role
        for j in range(local):
            pl.when(needed[j])(lambda j=j: copy(j).wait())


def load(levels, links, values):
    local = values.shape[1]
    return pl.pallas_call(
        load_kernel,
        name="load",
        out_shape=(
            jax.ShapeDtypeStruct((1,), jnp.int32),
            jax.ShapeDtypeStruct(values.shape[1:], BF16),
        ),
        in_specs=[SMEM, SMEM, HBM],
        out_specs=(SMEM, VMEM),
        scratch_shapes=[pltpu.SemaphoreType.DMA((local,))],
        cost_estimate=pl.CostEstimate(
            flops=0, bytes_accessed=local * BLK * BLK * 2, transcendentals=0
        ),
        compiler_params=pltpu.CompilerParams(vmem_limit_bytes=44 << 20),
    )(levels, links, values)


def multiply(kernel, levels, links, values, arrived, slots, scratch):
    group = len(arrived)
    local = values.shape[0]
    out = jax.ShapeDtypeStruct((slots,) + arrived[0].shape[1:], BF16)
    return pl.pallas_call(
        functools.partial(kernel, group),
        name=kernel.__name__,
        out_shape=(out,) * group,
        in_specs=[SMEM, SMEM, VMEM] + [VMEM] * group,
        out_specs=(VMEM,) * group,
        scratch_shapes=scratch,
        cost_estimate=pl.CostEstimate(
            flops=2 * local * 32 * BLK * BLK, bytes_accessed=2 * local * BLK * BLK, transcendentals=0
        ),
        compiler_params=pltpu.CompilerParams(vmem_limit_bytes=24 << 20),
    )(levels, links, values, *arrived)


def finish_kernel(role, group, level_ref, base_ref, held_ref, *refs):
    in_refs, out_ref, done_ref, sems = refs[:-3], refs[-3], refs[-2], refs[-1]
    _, _, _, upper_differs = place(level_ref)
    me = lax.axis_index("gy")
    parts = sems.shape[0]
    side, spacing, count = (
        (SC, spacing_coarse, HALF_C) if role == 1 else (SF, spacing_fine, HALF_F)
    )
    whole = count * BLK
    part = whole // parts
    centre = (side - 1) * 0.5

    def flush(index):
        start = index * part + jnp.where(upper_differs, 0, whole)
        at = pl.ds(pl.multiple_of(start, part), part)
        return pltpu.make_async_copy(
            done_ref.at[:, pl.ds(pl.multiple_of(index * part, part), part)],
            out_ref.at[:, at],
            sems.at[index],
        )

    first_plane = jnp.where(upper_differs, 0, side // 2)
    if role == 1:
        width = side * side
        for o in range(HALF_C):
            ghost = in_refs[0][o].astype(F32)
            for ref in in_refs[1:]:
                ghost = ghost + ref[o].astype(F32)
            for k in range(BLK // width):
                plane = lax.convert_element_type(first_plane + o * (BLK // width) + k, F32)
                push = cfl_ratio * spacing * jnp.abs(plane - centre)
                at = slice(o * BLK + k * width, o * BLK + (k + 1) * width)
                done_ref[:, at] = base_ref[:, at] + push * ghost[:, k * width : (k + 1) * width]
        flush(0).start()
        flush(0).wait()
        return

    offset = jnp.where(upper_differs, 0, HALF_F)
    for s, ref in zip(order(group), in_refs):
        local = ref.shape[0]
        first = peer(me, s, group) * local - offset

        @pl.when((first >= 0) & (first < HALF_F))
        def _(ref=ref, first=first, local=local):
            for j in range(local):
                slot = first + j
                plane = lax.convert_element_type(first_plane + slot // 2, F32)
                push = cfl_ratio * spacing * jnp.abs(plane - centre)
                at = pl.ds(pl.multiple_of(slot * BLK, BLK), BLK)
                done_ref[:, at] = base_ref[:, at] + push * ref[j].astype(F32)
            flush(lax.div(first, local)).start()

    for index in range(parts):
        flush(index).wait()


def finish(role, levels, base, held, arrived):
    group = len(arrived)
    rows_n = base.shape[0]
    parts = 1 if role == 1 else group // 2
    whole = NVC // 2 if role == 1 else NVF // 2
    return pl.pallas_call(
        functools.partial(finish_kernel, role, group),
        name="finish",
        out_shape=jax.ShapeDtypeStruct(held.shape, F32),
        in_specs=[SMEM, VMEM, HBM] + [VMEM] * group,
        out_specs=HBM,
        scratch_shapes=[pltpu.VMEM((rows_n, whole), F32), pltpu.SemaphoreType.DMA((parts,))],
        input_output_aliases={2: 0},
        cost_estimate=pl.CostEstimate(flops=10**6, bytes_accessed=10**6, transcendentals=0),
        compiler_params=pltpu.CompilerParams(vmem_limit_bytes=8 << 20),
    )(levels, base, held, *arrived)


def on_device(distribution, relax_rate, block_level, block_link, remap_values):
    blocks, group = lax.axis_size("gx"), lax.axis_size("gy")
    cells_y = distribution.shape[1]
    local = remap_values.shape[1]
    cells = distribution[0]

    def exchange(value, parity):
        pairs = []
        for low in range(parity, blocks - 1, 2):
            for y in range(group):
                here, there = low * group + y, (low + 1) * group + y
                pairs += [(here, there), (there, here)]
        return lax.ppermute(value, BOTH, pairs)

    everyone = range(group)

    def around(steps, outgoing, sources=everyone, targets=everyone, rows=False):
        arrived = []
        for s, value in zip(steps, outgoing):
            pairs = [
                (i, peer(i, s, group))
                for i in everyone
                if (i in sources and peer(i, s, group) in targets)
                or (rows and abs(i - peer(i, s, group)) == 1)
            ]
            arrived.append(lax.ppermute(value, "gy", pairs) if s and pairs else value)
        return arrived

    even, odd = prepare(block_level, block_link, cells)
    odd = exchange(odd, 1)
    even = exchange(even, 0)
    role, held = load(block_level, block_link, remap_values)
    edges = edge_rows(block_level, cells)

    def settle(level, rows):
        return relax(level, block_level, relax_rate, cells, even, odd, rows)

    def alone():
        left = lax.ppermute(edges[0], "gy", [(i, i + 1) for i in range(group - 1)])
        right = lax.ppermute(edges[1], "gy", [(i + 1, i) for i in range(group - 1)])
        return settle(None, [left, right])[0]

    def remapped(level, kernel, slots, scratch, arrived):
        made = multiply(kernel, block_level, block_link, held, arrived, slots, scratch)
        made = dict(zip(entry(group), made))
        return [made[s] for s in order(group)], settle(level, arrived[1:])

    def to_coarse(slots):
        outgoing = pieces(block_level, block_link, even, odd, edges, group, slots)
        sums = [pltpu.VMEM((HALF_C, group * cells_y, BLK), F32)]
        made, (out, base) = remapped(0, to_coarse_kernel, HALF_C, sums, around(entry(group), outgoing))
        return finish(1, block_level, base, out, around(order(group), made))

    def to_fine(active):
        outgoing = coarse_pieces(block_level, even, odd, edges, group)
        arrived = around(entry(group), outgoing, targets=active, rows=True)
        made, (out, base) = remapped(1, to_fine_kernel, local, [], arrived)
        return finish(2, block_level, base, out, around(order(group), made, sources=active))

    branches = [alone]
    for slots in sizes(local):
        branches.append(functools.partial(to_coarse, slots))
    for active in (range(group // 2, group), range(group // 2)):
        branches.append(functools.partial(to_fine, active))
    updated = lax.switch(role[0], branches)
    return updated[None]


def solution(mesh):
    in_specs = (P("gx", "gy", None), P("gx", "gy"), P(), P(), P(None, "gy", None, None))
    out_specs = P("gx", "gy", None)
    return jax.shard_map(
        on_device, mesh=mesh, in_specs=in_specs, out_specs=out_specs, check_vma=False
    )
```

profile of v0, /device:TPU:4, one launch (start us, length us, event | category | flops | bytes accessed | tf_op | source)
XLA Modules:
  0.0 38.9 jit_solution(10342382505458150604)
XLA Ops:
  0.0 0.0 copy-start.1
  0.0 0.0 copy-start.2
  0.0 0.0 copy-start
  0.0 0.0 copy-start.3
  0.0 1.4 %prepare.1 = (bf16[32,8,512]{2,1,0:T(8,128)(2,1)S(1)}, bf16[32,8,512]{2,1,0:T(8,128)(2,1)S(1)}) custom-call(s32[8]{0:T(128)} %level_ref.5, s32[2,64]{1,0:T(2,128)} %link_ref.3, f32[8,32768]{1,0:T(8,128)} %bitcast.8), custom_call_target="tpu_custom_call" | custom-call | flops 1000000 | bytes 2000000 | tf_op jit(solution)/shard_map/prepare/pallas_call | solution.py:111
  1.4 0.3 collective-permute-start.32
  1.8 3.2 %collective-permute-start.33 = (bf16[32,8,512]{2,1,0:T(8,128)(2,1)S(1)}, bf16[32,8,512]{2,1,0:T(8,128)(2,1)S(1)}, u32[]{:S(2)}, u32[]{:S(2)}) collective-permute-start(bf16[32,8,512]{2,1,0:T(8,128)(2,1)S(1)} %get-tuple-element.229), channel_id=1, source_target_pairs={{4,8},{8,4},{5,9},{9,5},{6,10},{10,6},{7,11},{11,7},{12,16},{16,12... | collective-permute-start | bytes 786440 | tf_op jit(solution)/shard_map/ppermute | solution.py:666
  4.9 3.1 %load.1 = (s32[1]{0:T(128)}, bf16[16,512,512]{2,1,0:T(8,128)(2,1)S(1)}) custom-call(s32[8]{0:T(128)} %level_ref.5, s32[2,64]{1,0:T(2,128)} %link_ref.3, bf16[2,16,512,512]{3,2,1,0:T(8,128)(2,1)} %values_ref.1), custom_call_target="tpu_custom_call" | custom-call | bytes 8388608 | tf_op jit(solution)/shard_map/load/pallas_call | solution.py:545
  8.7 0.0 copy-done.1
  8.7 0.0 copy-done
  8.7 0.6 %edge_rows.1 = (bf16[32,512]{1,0:T(8,128)(2,1)S(1)}, bf16[32,512]{1,0:T(8,128)(2,1)S(1)}) custom-call(s32[8]{0:T(128)S(1)} %copy-done.1, f32[8,32768]{1,0:T(8,128)S(1)} %bitcast.9), custom_call_target="tpu_custom_call" | custom-call | flops 1000000 | bytes 2000000 | tf_op jit(solution)/shard_map/edge_rows/pallas_call | solution.py:148
  9.3 0.0 collective-permute-done.32
  9.3 2.7 %collective-permute-done.33 = bf16[32,8,512]{2,1,0:T(8,128)(2,1)S(1)} collective-permute-done((bf16[32,8,512]{2,1,0:T(8,128)(2,1)S(1)}, bf16[32,8,512]{2,1,0:T(8,128)(2,1)S(1)}, u32[]{:S(2)}, u32[]{:S(2)}) %collective-permute-start.33) | collective-permute-done | bytes 262176 | tf_op jit(solution)/shard_map/ppermute | solution.py:666
  12.0 0.0 copy-done.2
  12.0 0.0 copy-done.3
  12.0 26.7 %conditional.1 = (f32[1,8,32768]{2,1,0:T(8,128)}) conditional(s32[]{:T(128)} %bitcast.6, (bf16[32,512]{1,0:T(8,128)(2,1)S(1)}, bf16[32,512]{1,0:T(8,128)(2,1)S(1)}, s32[8]{0:T(128)S(1)}, f32[1,8]{1,0:T(1,128)S(1)}, f32[8,32768]{1,0:T(8,128)S(1)}, /*index=5*/bf16[32,8,512]{2,1,0:T(8,128)(2,1)S(1)}, ...), branch_computations={%region_0.0_spmd, %region_1.0_spmd, %region_2.0_spmd, %region_3.0_... | conditional | flops 279535456 | bytes 17141368 | solution.py:718
  12.0 1.0 %pieces.3 = (bf16[10,8,512]{2,1,0:T(8,128)(2,1)S(1)}, bf16[14,8,512]{2,1,0:T(8,128)(2,1)S(1)}, bf16[14,8,512]{2,1,0:T(8,128)(2,1)S(1)}, bf16[14,8,512]{2,1,0:T(8,128)(2,1)S(1)}) custom-call(s32[8]{0:T(128)S(1)} %get-tuple-element.124.level_ref, s32[2,64]{1,0:T(2,128)S(1)} %get-tuple-element.129.link_ref, ...), custom_call_target="tpu_custom_call" | custom-call | flops 100000 | bytes 1000000 | tf_op jit(solution)/shard_map/cond/branch_1_fun/pieces/pallas_call | solution.py:439
  13.0 3.3 %collective-permute-start.2 = (bf16[14,8,512]{2,1,0:T(8,128)(2,1)S(1)}, bf16[14,8,512]{2,1,0:T(8,128)(2,1)S(1)}, u32[]{:S(2)}, u32[]{:S(2)}) collective-permute-start(bf16[14,8,512]{2,1,0:T(8,128)(2,1)S(1)} %get-tuple-element.132), channel_id=1, source_target_pairs={{0,2},{1,3},{2,0},{3,1},{4,6},{5,7},{6,4},{7,5},{8,10},{9,11},{10,... | collective-permute-start | bytes 344072 | tf_op jit(solution)/shard_map/cond/branch_1_fun/ppermute | solution.py:679
  16.3 1.6 %collective-permute-start.3 = (bf16[14,8,512]{2,1,0:T(8,128)(2,1)S(1)}, bf16[14,8,512]{2,1,0:T(8,128)(2,1)S(1)}, u32[]{:S(2)}, u32[]{:S(2)}) collective-permute-start(bf16[14,8,512]{2,1,0:T(8,128)(2,1)S(1)} %get-tuple-element.133), channel_id=1, source_target_pairs={{0,1},{1,0},{2,3},{3,2},{4,5},{5,4},{6,7},{7,6},{8,9},{9,8},{10,11... | collective-permute-start | bytes 344072 | tf_op jit(solution)/shard_map/cond/branch_1_fun/ppermute | solution.py:679
  17.9 0.0 collective-permute-start.4
  17.9 1.7 %collective-permute-done.2.refs_0_.refs_1_ = bf16[14,8,512]{2,1,0:T(8,128)(2,1)S(1)} collective-permute-done((bf16[14,8,512]{2,1,0:T(8,128)(2,1)S(1)}, bf16[14,8,512]{2,1,0:T(8,128)(2,1)S(1)}, u32[]{:S(2)}, u32[]{:S(2)}) %collective-permute-start.2) | collective-permute-done | bytes 114720 | tf_op jit(solution)/shard_map/cond/branch_1_fun/ppermute | solution.py:679
  19.6 2.5 %collective-permute-done.3.refs_1_.refs_2_ = bf16[14,8,512]{2,1,0:T(8,128)(2,1)S(1)} collective-permute-done((bf16[14,8,512]{2,1,0:T(8,128)(2,1)S(1)}, bf16[14,8,512]{2,1,0:T(8,128)(2,1)S(1)}, u32[]{:S(2)}, u32[]{:S(2)}) %collective-permute-start.3) | collective-permute-done | bytes 114720 | tf_op jit(solution)/shard_map/cond/branch_1_fun/ppermute | solution.py:679
  22.0 2.5 %collective-permute-done.4.refs_2_.refs_3_ = bf16[14,8,512]{2,1,0:T(8,128)(2,1)S(1)} collective-permute-done((bf16[14,8,512]{2,1,0:T(8,128)(2,1)S(1)}, bf16[14,8,512]{2,1,0:T(8,128)(2,1)S(1)}, u32[]{:S(2)}, u32[]{:S(2)}) %collective-permute-start.4) | collective-permute-done | bytes 114720 | tf_op jit(solution)/shard_map/cond/branch_1_fun/ppermute | solution.py:679
  24.6 1.7 %to_coarse_kernel.3 = (bf16[4,8,512]{2,1,0:T(8,128)(2,1)S(1)}, bf16[4,8,512]{2,1,0:T(8,128)(2,1)S(1)}, bf16[4,8,512]{2,1,0:T(8,128)(2,1)S(1)}, bf16[4,8,512]{2,1,0:T(8,128)(2,1)S(1)}) custom-call(s32[8]{0:T(128)S(1)} %get-tuple-element.124.level_ref, s32[2,64]{1,0:T(2,128)S(1)} %get-tuple-element.129.link_ref, ...), custom_call_target="tpu_custom_call" | custom-call | flops 268435456 | bytes 8388608 | tf_op jit(solution)/shard_map/cond/branch_1_fun/to_coarse_kernel/pallas_call | solution.py:566
  26.2 5.2 %collective-permute-start.5 = (bf16[4,8,512]{2,1,0:T(8,128)(2,1)S(1)}, bf16[4,8,512]{2,1,0:T(8,128)(2,1)S(1)}, u32[]{:S(2)}, u32[]{:S(2)}) collective-permute-start(bf16[4,8,512]{2,1,0:T(8,128)(2,1)S(1)} %get-tuple-element.140), channel_id=1, source_target_pairs={{0,2},{1,3},{2,0},{3,1},{4,6},{5,7},{6,4},{7,5},{8,10},{9,11},{10,... | collective-permute-start | bytes 98312 | tf_op jit(solution)/shard_map/cond/branch_1_fun/ppermute | solution.py:679
  31.4 0.2 collective-permute-start.6
  31.7 0.4 %collective-permute-start.7 = (bf16[4,8,512]{2,1,0:T(8,128)(2,1)S(1)}, bf16[4,8,512]{2,1,0:T(8,128)(2,1)S(1)}, u32[]{:S(2)}, u32[]{:S(2)}) collective-permute-start(bf16[4,8,512]{2,1,0:T(8,128)(2,1)S(1)} %get-tuple-element.142), channel_id=1, source_target_pairs={{0,1},{1,0},{2,3},{3,2},{4,5},{5,4},{6,7},{7,6},{8,9},{9,8},{10,11... | collective-permute-start | bytes 98312 | tf_op jit(solution)/shard_map/cond/branch_1_fun/ppermute | solution.py:679
  32.1 1.8 %relax.7 = (f32[8,32768]{1,0:T(8,128)}, f32[8,2048]{1,0:T(8,128)S(1)}) custom-call(s32[8]{0:T(128)S(1)} %get-tuple-element.124.level_ref, f32[1,8]{1,0:T(1,128)S(1)} %get-tuple-element.125.rate_ref, f32[8,32768]{1,0:T(8,128)S(1)} %get-tuple-element.126.cells_ref, bf16[32,8,512]{2,1,0:T(8,128)(2,1)S(1)} %get-tuple-element.127.even_ref, ...), custom_call_target="tpu_custom_call" | custom-call | flops 10000000 | bytes 4000000 | tf_op jit(solution)/shard_map/cond/branch_1_fun/relax/pallas_call | solution.py:341
  33.9 2.1 %collective-permute-done.5.refs_1_ = bf16[4,8,512]{2,1,0:T(8,128)(2,1)S(1)} collective-permute-done((bf16[4,8,512]{2,1,0:T(8,128)(2,1)S(1)}, bf16[4,8,512]{2,1,0:T(8,128)(2,1)S(1)}, u32[]{:S(2)}, u32[]{:S(2)}) %collective-permute-start.5) | collective-permute-done | bytes 32800 | tf_op jit(solution)/shard_map/cond/branch_1_fun/ppermute | solution.py:679
  36.0 1.2 %collective-permute-done.6.refs_2_ = bf16[4,8,512]{2,1,0:T(8,128)(2,1)S(1)} collective-permute-done((bf16[4,8,512]{2,1,0:T(8,128)(2,1)S(1)}, bf16[4,8,512]{2,1,0:T(8,128)(2,1)S(1)}, u32[]{:S(2)}, u32[]{:S(2)}) %collective-permute-start.6) | collective-permute-done | bytes 32800 | tf_op jit(solution)/shard_map/cond/branch_1_fun/ppermute | solution.py:679
  37.3 0.0 collective-permute-done.7.refs_3_
  37.3 1.2 %finish.5 = f32[8,32768]{1,0:T(8,128)} custom-call(s32[8]{0:T(128)S(1)} %get-tuple-element.124.level_ref, f32[8,2048]{1,0:T(8,128)S(1)} %get-tuple-element.135.base_ref, f32[8,32768]{1,0:T(8,128)} %get-tuple-element.136.held_ref, bf16[4,8,512]{2,1,0:T(8,128)(2,1)S(1)} %get-tuple-element.139.refs_0_, ...), custom_call_target="tpu_custom_call", output_to_operand_aliasing={{}: (2, {})} | custom-call | flops 1000000 | bytes 1000000 | tf_op jit(solution)/shard_map/cond/branch_1_fun/finish/pallas_call | solution.py:641
Async XLA Ops:
  0.0 8.7 %copy-start.1 = (s32[8]{0:T(128)S(1)}, s32[8]{0:T(128)}, u32[]{:S(2)}) copy-start(s32[8]{0:T(128)} %level_ref.5) | copy-start | bytes 100
  0.0 12.0 %copy-start.2 = (s32[2,64]{1,0:T(2,128)S(1)}, s32[2,64]{1,0:T(2,128)}, u32[]{:S(2)}) copy-start(s32[2,64]{1,0:T(2,128)} %link_ref.3) | copy-start | bytes 1540
  0.0 8.7 %copy-start = (f32[1,8,32768]{2,1,0:T(8,128)S(1)}, f32[1,8,32768]{2,1,0:T(8,128)}, u32[]{:S(2)}) copy-start(f32[1,8,32768]{2,1,0:T(8,128)} %param.11) | copy-start | bytes 3145732
  0.0 12.0 %copy-start.3 = (f32[1,8]{1,0:T(1,128)S(1)}, f32[1,8]{1,0:T(1,128)}, u32[]{:S(2)}) copy-start(f32[1,8]{1,0:T(1,128)} %param.12) | copy-start | bytes 100
  1.4 7.9 %collective-permute-start.32 = (bf16[32,8,512]{2,1,0:T(8,128)(2,1)S(1)}, bf16[32,8,512]{2,1,0:T(8,128)(2,1)S(1)}, u32[]{:S(2)}, u32[]{:S(2)}) collective-permute-start(bf16[32,8,512]{2,1,0:T(8,128)(2,1)S(1)} %get-tuple-element.228), channel_id=1, source_target_pairs={{0,4},{4,0},{1,5},{5,1},{2,6},{6,2},{3,7},{7,3},{8,12},{12,8},{9,1... | collective-permute-start | bytes 786440 | tf_op jit(solution)/shard_map/ppermute | solution.py:666
  1.8 10.2 %collective-permute-start.33 = (bf16[32,8,512]{2,1,0:T(8,128)(2,1)S(1)}, bf16[32,8,512]{2,1,0:T(8,128)(2,1)S(1)}, u32[]{:S(2)}, u32[]{:S(2)}) collective-permute-start(bf16[32,8,512]{2,1,0:T(8,128)(2,1)S(1)} %get-tuple-element.229), channel_id=1, source_target_pairs={{4,8},{8,4},{5,9},{9,5},{6,10},{10,6},{7,11},{11,7},{12,16},{16,12... | collective-permute-start | bytes 786440 | tf_op jit(solution)/shard_map/ppermute | solution.py:666
  13.0 6.6 %collective-permute-start.2 = (bf16[14,8,512]{2,1,0:T(8,128)(2,1)S(1)}, bf16[14,8,512]{2,1,0:T(8,128)(2,1)S(1)}, u32[]{:S(2)}, u32[]{:S(2)}) collective-permute-start(bf16[14,8,512]{2,1,0:T(8,128)(2,1)S(1)} %get-tuple-element.132), channel_id=1, source_target_pairs={{0,2},{1,3},{2,0},{3,1},{4,6},{5,7},{6,4},{7,5},{8,10},{9,11},{10,... | collective-permute-start | bytes 344072 | tf_op jit(solution)/shard_map/cond/branch_1_fun/ppermute | solution.py:679
  16.3 5.8 %collective-permute-start.3 = (bf16[14,8,512]{2,1,0:T(8,128)(2,1)S(1)}, bf16[14,8,512]{2,1,0:T(8,128)(2,1)S(1)}, u32[]{:S(2)}, u32[]{:S(2)}) collective-permute-start(bf16[14,8,512]{2,1,0:T(8,128)(2,1)S(1)} %get-tuple-element.133), channel_id=1, source_target_pairs={{0,1},{1,0},{2,3},{3,2},{4,5},{5,4},{6,7},{7,6},{8,9},{9,8},{10,11... | collective-permute-start | bytes 344072 | tf_op jit(solution)/shard_map/cond/branch_1_fun/ppermute | solution.py:679
  17.9 6.7 %collective-permute-start.4 = (bf16[14,8,512]{2,1,0:T(8,128)(2,1)S(1)}, bf16[14,8,512]{2,1,0:T(8,128)(2,1)S(1)}, u32[]{:S(2)}, u32[]{:S(2)}) collective-permute-start(bf16[14,8,512]{2,1,0:T(8,128)(2,1)S(1)} %get-tuple-element.134), channel_id=1, source_target_pairs={{0,3},{1,2},{2,1},{3,0},{4,7},{5,6},{6,5},{7,4},{8,11},{9,10},{10,... | collective-permute-start | bytes 344072 | tf_op jit(solution)/shard_map/cond/branch_1_fun/ppermute | solution.py:679
  26.2 9.8 %collective-permute-start.5 = (bf16[4,8,512]{2,1,0:T(8,128)(2,1)S(1)}, bf16[4,8,512]{2,1,0:T(8,128)(2,1)S(1)}, u32[]{:S(2)}, u32[]{:S(2)}) collective-permute-start(bf16[4,8,512]{2,1,0:T(8,128)(2,1)S(1)} %get-tuple-element.140), channel_id=1, source_target_pairs={{0,2},{1,3},{2,0},{3,1},{4,6},{5,7},{6,4},{7,5},{8,10},{9,11},{10,... | collective-permute-start | bytes 98312 | tf_op jit(solution)/shard_map/cond/branch_1_fun/ppermute | solution.py:679
  31.4 5.8 %collective-permute-start.6 = (bf16[4,8,512]{2,1,0:T(8,128)(2,1)S(1)}, bf16[4,8,512]{2,1,0:T(8,128)(2,1)S(1)}, u32[]{:S(2)}, u32[]{:S(2)}) collective-permute-start(bf16[4,8,512]{2,1,0:T(8,128)(2,1)S(1)} %get-tuple-element.141), channel_id=1, source_target_pairs={{0,3},{1,2},{2,1},{3,0},{4,7},{5,6},{6,5},{7,4},{8,11},{9,10},{10,... | collective-permute-start | bytes 98312 | tf_op jit(solution)/shard_map/cond/branch_1_fun/ppermute | solution.py:679
  31.7 5.6 %collective-permute-start.7 = (bf16[4,8,512]{2,1,0:T(8,128)(2,1)S(1)}, bf16[4,8,512]{2,1,0:T(8,128)(2,1)S(1)}, u32[]{:S(2)}, u32[]{:S(2)}) collective-permute-start(bf16[4,8,512]{2,1,0:T(8,128)(2,1)S(1)} %get-tuple-element.142), channel_id=1, source_target_pairs={{0,1},{1,0},{2,3},{3,2},{4,5},{5,4},{6,7},{7,6},{8,9},{9,8},{10,11... | collective-permute-start | bytes 98312 | tf_op jit(solution)/shard_map/cond/branch_1_fun/ppermute | solution.py:679
where the time goes:
time: 39.7 us; the launch traced here: 38.9 us
  starting transfers between devices  14.2 us (36%)
  waiting for transfers between devices  12.7 us (32%)
  Pallas kernels  10.7 us (27%)
  between operations  0.9 us (2%)
    ppermute x6, starting transfers between devices, around(): arrived.append(lax.ppermute(value, 'gy', pairs) if s and pairs else value)  10.7 us
    ppermute x6, waiting for transfers between devices, around(): arrived.append(lax.ppermute(value, 'gy', pairs) if s and pairs else value)  10.1 us
    ppermute x2, starting transfers between devices, exchange(): return lax.ppermute(value, BOTH, pairs)  3.51 us
    pallas_call x1, Pallas kernels, load(): pl.pallas_call(load_kernel, name='load', out_shape=(jax.ShapeDtypeStruct(...  3.1 us
    ppermute x2, waiting for transfers between devices, exchange(): return lax.ppermute(value, BOTH, pairs)  2.68 us
    pallas_call x1, Pallas kernels, relax(): pl.pallas_call(functools.partial(relax_kernel, level), name='relax', out_...  1.8 us
    pallas_call x1, Pallas kernels, multiply(): pl.pallas_call(functools.partial(kernel, group), name=kernel.__name__, ou...  1.66 us
    pallas_call x1, Pallas kernels, prepare(): pl.pallas_call(prepare_kernel, name='prepare', out_shape=(half, half), in...  1.4 us
  transfers between devices with their start and end apart: 8, of which 6 were waited for; matrix products, arithmetic and copies ran while one was open for 0% of the time, Pallas kernels for 14%

commit v1 on v0

--- a/solution.py
+++ b/solution.py
@@ -51,7 +51,7 @@
 
 
 def entry(group):
-    return sorted(range(group), key=lambda s: (s > 0, s == group - 1, s != group // 2, s))
+    return order(group)
 
 
 def near(group):
@@ -293,9 +293,7 @@
     else:
         side_ref[...] = jnp.zeros_like(side_ref)
         me, group = lax.axis_index("gy"), lax.axis_size("gy")
-        for s, ref in zip(entry(group)[1:], row_refs):
-            if s not in near(group):
-                continue
+        for s, ref in zip(near(group), row_refs):
             first = ref.shape[0] - ROWS
             for k, by in ((0, -1), (1, 1)):
 
@@ -371,9 +369,8 @@
                     out_ref[first + j] = source_ref[8 * j : 8 * j + 8, :]
 
 
-def coarse_kernel(group, level_ref, even_ref, odd_ref, ahead_ref, back_ref, *out_refs):
-    block, _, lower_differs, _ = place(level_ref)
-    use_even = (block % 2 == 0) != lower_differs
+def coarse_kernel(group, from_lower, even_ref, odd_ref, ahead_ref, back_ref, *out_refs):
+    use_even = (lax.axis_index("gx") % 2 == 0) != from_lower
     for j in range(VBC):
         a, b = even_ref[j].astype(F32), odd_ref[j].astype(F32)
         piece = jnp.where(use_even, a, b).astype(BF16)
@@ -418,21 +415,21 @@
 
 def outgoing_shapes(slots, group, rows_n):
     return tuple(
-        jax.ShapeDtypeStruct((slots + (ROWS if s else 0), rows_n, BLK), BF16)
+        jax.ShapeDtypeStruct((slots + (ROWS if s in near(group) else 0), rows_n, BLK), BF16)
         for s in entry(group)
     )
 
 
-def coarse_pieces(levels, even, odd, edges, group):
+def coarse_pieces(from_lower, even, odd, edges, group):
     return pl.pallas_call(
-        functools.partial(coarse_kernel, group),
+        functools.partial(coarse_kernel, group, from_lower),
         name="coarse_pieces",
         out_shape=outgoing_shapes(VBC, group, even.shape[1]),
-        in_specs=[SMEM] + [VMEM] * 4,
+        in_specs=[VMEM] * 4,
         out_specs=(VMEM,) * group,
         cost_estimate=pl.CostEstimate(flops=10**5, bytes_accessed=10**6, transcendentals=0),
         compiler_params=pltpu.CompilerParams(vmem_limit_bytes=8 << 20),
-    )(levels, even, odd, *edges)
+    )(even, odd, *edges)
 
 
 def pieces(levels, links, even, odd, edges, group, slots):
@@ -452,10 +449,11 @@
     return jnp.concatenate([ref[index].astype(F32) for ref in refs], axis=0).astype(BF16)
 
 
-def to_coarse_kernel(group, level_ref, link_ref, values_ref, *refs):
+def to_coarse_kernel(group, level_ref, link_ref, head_ref, tail_ref, *refs):
     in_refs, out_refs, sum_ref = refs[:group], refs[group : 2 * group], refs[-1]
     _, _, lower_differs, _ = place(level_ref)
-    local = values_ref.shape[0]
+    half = head_ref.shape[0]
+    local = half + tail_ref.shape[0]
     cells_y = in_refs[0].shape[1]
     first = lax.axis_index("gy") * local
     offset = jnp.where(lower_differs, HALF_C, 0)
@@ -469,7 +467,7 @@
         @pl.when(needed[j])
         def _(j=j, slot=slot):
             sum_ref[targets[j]] += jnp.dot(
-                stacked(in_refs, slot), values_ref[j], preferred_element_type=F32
+                stacked(in_refs, slot), (head_ref[j] if j < half else tail_ref[j - half]), preferred_element_type=F32
             )
 
         slot = slot + needed[j].astype(jnp.int32)
@@ -477,10 +475,11 @@
         out_ref[...] = sum_ref[:, s * cells_y : (s + 1) * cells_y, :].astype(BF16)
 
 
-def to_fine_kernel(group, level_ref, link_ref, values_ref, *refs):
+def to_fine_kernel(group, level_ref, link_ref, head_ref, tail_ref, *refs):
     in_refs, out_refs = refs[:group], refs[group : 2 * group]
     _, _, lower_differs, _ = place(level_ref)
-    local = values_ref.shape[0]
+    half = head_ref.shape[0]
+    local = half + tail_ref.shape[0]
     cells_y = in_refs[0].shape[1]
     first = lax.axis_index("gy") * local
     active = (first >= HALF_F) == lower_differs
@@ -490,45 +489,44 @@
         for j in range(local):
             product = jnp.dot(
                 stacked(in_refs, link_ref[0, first + j]),
-                values_ref[j],
+                (head_ref[j] if j < half else tail_ref[j - half]),
                 preferred_element_type=F32,
             ).astype(BF16)
             for s, out_ref in enumerate(out_refs):
                 out_ref[j] = product[s * cells_y : (s + 1) * cells_y, :]
 
 
-def load_kernel(level_ref, link_ref, values_ref, role_ref, held_ref, sems):
+def load_kernel(start, stop, level_ref, link_ref, values_ref, role_ref, held_ref, sems):
     _, own, lower_differs, upper_differs = place(level_ref)
     local = values_ref.shape[1]
     first = lax.axis_index("gy") * local
     fine = own == 1
+    source = jnp.where(fine, 0, 1)
     differs = lower_differs | upper_differs
+
+    def needed(j):
+        coarse = (link_ref[1, first + j] >= HALF_C) == lower_differs
+        here = jnp.where(fine, (first >= HALF_F) == lower_differs, coarse)
+        return here & differs
+
+    def copy(j):
+        at = j - start
+        return pltpu.make_async_copy(values_ref.at[source, j], held_ref.at[at], sems.at[at])
+
+    for j in range(start, stop):
+        pl.when(needed(j))(lambda j=j: copy(j).start())
+
     counts = sizes(local)
     fine_role = len(counts) + jnp.where(lower_differs, 1, 2)
     role_ref[0] = jnp.where(differs & fine, fine_role, 0)
 
-    @pl.when(differs & fine & ((first >= HALF_F) == lower_differs))
+    @pl.when(differs & jnp.logical_not(fine) & (start == 0))
     def _():
-        whole = pltpu.make_async_copy(values_ref.at[0], held_ref, sems.at[0])
-        whole.start()
-        whole.wait()
-
-    @pl.when(differs & jnp.logical_not(fine))
-    def _():
-        def hit(f):
-            return (link_ref[1, f] >= HALF_C) == lower_differs
-
-        def copy(j):
-            return pltpu.make_async_copy(values_ref.at[1, j], held_ref.at[j], sems.at[j])
-
-        needed = [hit(first + j) for j in range(local)]
-        for j in range(local):
-            pl.when(needed[j])(lambda j=j: copy(j).start())
-
         def most(h, worst):
             count = jnp.int32(0)
             for j in range(local):
-                count = count + hit(h * local + j).astype(jnp.int32)
+                hit = (link_ref[1, h * local + j] >= HALF_C) == lower_differs
+                count = count + hit.astype(jnp.int32)
             return jnp.maximum(worst, count)
 
         worst = lax.fori_loop(0, VBF // local, most, jnp.int32(0))
@@ -536,24 +534,24 @@
         for size in counts[:-1]:
             role = role + (worst > size).astype(jnp.int32)
         role_ref[0] = role
-        for j in range(local):
-            pl.when(needed[j])(lambda j=j: copy(j).wait())
-
-
-def load(levels, links, values):
-    local = values.shape[1]
+
+    for j in range(start, stop):
+        pl.when(needed(j))(lambda j=j: copy(j).wait())
+
+
+def load(levels, links, values, start, stop):
     return pl.pallas_call(
-        load_kernel,
+        functools.partial(load_kernel, start, stop),
         name="load",
         out_shape=(
             jax.ShapeDtypeStruct((1,), jnp.int32),
-            jax.ShapeDtypeStruct(values.shape[1:], BF16),
+            jax.ShapeDtypeStruct((stop - start,) + values.shape[2:], BF16),
         ),
         in_specs=[SMEM, SMEM, HBM],
         out_specs=(SMEM, VMEM),
-        scratch_shapes=[pltpu.SemaphoreType.DMA((local,))],
+        scratch_shapes=[pltpu.SemaphoreType.DMA((stop - start,))],
         cost_estimate=pl.CostEstimate(
-            flops=0, bytes_accessed=local * BLK * BLK * 2, transcendentals=0
+            flops=0, bytes_accessed=(stop - start) * BLK * BLK * 2, transcendentals=0
         ),
         compiler_params=pltpu.CompilerParams(vmem_limit_bytes=44 << 20),
     )(levels, links, values)
@@ -561,25 +559,29 @@
 
 def multiply(kernel, levels, links, values, arrived, slots, scratch):
     group = len(arrived)
-    local = values.shape[0]
+    local = sum(part.shape[0] for part in values)
     out = jax.ShapeDtypeStruct((slots,) + arrived[0].shape[1:], BF16)
     return pl.pallas_call(
         functools.partial(kernel, group),
         name=kernel.__name__,
         out_shape=(out,) * group,
-        in_specs=[SMEM, SMEM, VMEM] + [VMEM] * group,
+        in_specs=[SMEM, SMEM, VMEM, VMEM] + [VMEM] * group,
         out_specs=(VMEM,) * group,
         scratch_shapes=scratch,
         cost_estimate=pl.CostEstimate(
             flops=2 * local * 32 * BLK * BLK, bytes_accessed=2 * local * BLK * BLK, transcendentals=0
         ),
         compiler_params=pltpu.CompilerParams(vmem_limit_bytes=24 << 20),
-    )(levels, links, values, *arrived)
-
-
-def finish_kernel(role, group, level_ref, base_ref, held_ref, *refs):
-    in_refs, out_ref, done_ref, sems = refs[:-3], refs[-3], refs[-2], refs[-1]
-    _, _, _, upper_differs = place(level_ref)
+    )(levels, links, *values, *arrived)
+
+
+def finish_kernel(role, group, from_lower, *refs):
+    if from_lower is None:
+        upper_differs, refs = place(refs[0])[3], refs[1:]
+    else:
+        upper_differs = not from_lower
+    base_ref, in_refs = refs[0], refs[2:-3]
+    out_ref, done_ref, sems = refs[-3:]
     me = lax.axis_index("gy")
     parts = sems.shape[0]
     side, spacing, count = (
@@ -615,6 +617,7 @@
         return
 
     offset = jnp.where(upper_differs, 0, HALF_F)
+    per = HALF_F // parts
     for s, ref in zip(order(group), in_refs):
         local = ref.shape[0]
         first = peer(me, s, group) * local - offset
@@ -623,32 +626,35 @@
         def _(ref=ref, first=first, local=local):
             for j in range(local):
                 slot = first + j
+                if j and j % per == 0:
+                    flush(lax.div(slot, per) - 1).start()
                 plane = lax.convert_element_type(first_plane + slot // 2, F32)
                 push = cfl_ratio * spacing * jnp.abs(plane - centre)
                 at = pl.ds(pl.multiple_of(slot * BLK, BLK), BLK)
                 done_ref[:, at] = base_ref[:, at] + push * ref[j].astype(F32)
-            flush(lax.div(first, local)).start()
+            flush(lax.div(first + local, per) - 1).start()
 
     for index in range(parts):
         flush(index).wait()
 
 
-def finish(role, levels, base, held, arrived):
+def finish(role, from_lower, levels, base, held, arrived):
     group = len(arrived)
     rows_n = base.shape[0]
-    parts = 1 if role == 1 else group // 2
+    parts = 1 if role == 1 else HALF_F // min(4, VBF // group)
     whole = NVC // 2 if role == 1 else NVF // 2
+    scalars = [levels] if from_lower is None else []
     return pl.pallas_call(
-        functools.partial(finish_kernel, role, group),
+        functools.partial(finish_kernel, role, group, from_lower),
         name="finish",
         out_shape=jax.ShapeDtypeStruct(held.shape, F32),
-        in_specs=[SMEM, VMEM, HBM] + [VMEM] * group,
+        in_specs=[SMEM] * len(scalars) + [VMEM, HBM] + [VMEM] * group,
         out_specs=HBM,
         scratch_shapes=[pltpu.VMEM((rows_n, whole), F32), pltpu.SemaphoreType.DMA((parts,))],
-        input_output_aliases={2: 0},
+        input_output_aliases={len(scalars) + 1: 0},
         cost_estimate=pl.CostEstimate(flops=10**6, bytes_accessed=10**6, transcendentals=0),
         compiler_params=pltpu.CompilerParams(vmem_limit_bytes=8 << 20),
-    )(levels, base, held, *arrived)
+    )(*scalars, base, held, *arrived)
 
 
 def on_device(distribution, relax_rate, block_level, block_link, remap_values):
@@ -682,7 +688,7 @@
     even, odd = prepare(block_level, block_link, cells)
     odd = exchange(odd, 1)
     even = exchange(even, 0)
-    role, held = load(block_level, block_link, remap_values)
+    role, head = load(block_level, block_link, remap_values, 0, local // 2)
     edges = edge_rows(block_level, cells)
 
     def settle(level, rows):
@@ -694,21 +700,23 @@
         return settle(None, [left, right])[0]
 
     def remapped(level, kernel, slots, scratch, arrived):
-        made = multiply(kernel, block_level, block_link, held, arrived, slots, scratch)
+        tail = load(block_level, block_link, remap_values, local // 2, local)[1]
+        values = [head, tail]
+        made = multiply(kernel, block_level, block_link, values, arrived, slots, scratch)
         made = dict(zip(entry(group), made))
-        return [made[s] for s in order(group)], settle(level, arrived[1:])
+        return [made[s] for s in order(group)], settle(level, [p for s, p in zip(entry(group), arrived) if s in near(group)])
 
     def to_coarse(slots):
         outgoing = pieces(block_level, block_link, even, odd, edges, group, slots)
         sums = [pltpu.VMEM((HALF_C, group * cells_y, BLK), F32)]
         made, (out, base) = remapped(0, to_coarse_kernel, HALF_C, sums, around(entry(group), outgoing))
-        return finish(1, block_level, base, out, around(order(group), made))
+        return finish(1, None, block_level, base, out, around(order(group), made))
 
     def to_fine(active):
-        outgoing = coarse_pieces(block_level, even, odd, edges, group)
+        outgoing = coarse_pieces(active[0] > 0, even, odd, edges, group)
         arrived = around(entry(group), outgoing, targets=active, rows=True)
         made, (out, base) = remapped(1, to_fine_kernel, local, [], arrived)
-        return finish(2, block_level, base, out, around(order(group), made, sources=active))
+        return finish(2, active[0] > 0, block_level, base, out, around(order(group), made, sources=active))
 
     branches = [alone]
     for slots in sizes(local):

time: 39.7 us -> 37.9 us (0.955); the launches traced: 38.9 us -> 38.2 us
  waiting for transfers between devices: 12.7 us -> 7.65 us
  Pallas kernels: 10.7 us -> 14.5 us
  starting transfers between devices: 14.2 us -> 14.9 us
    ppermute x6, waiting for transfers between devices: 10.1 us -> 5.34 us  [around(): arrived.append(lax.ppermute(value, 'gy', pairs) if s and pairs else value)]
    pallas_call x3 -> x4, Pallas kernels: 5.27 us -> 7.85 us  [the longest x2 6.79 us: load(): pl.pallas_call(functools.partial(load_kernel, start, stop), name='load',...]
    ppermute x6, starting transfers between devices: 10.7 us -> 11.3 us  [around(): arrived.append(lax.ppermute(value, 'gy', pairs) if s and pairs else value)]
    pallas_call x1, Pallas kernels: 1.66 us -> 2.11 us  [multiply(): pl.pallas_call(functools.partial(kernel, group), name=kernel.__name__, ou...]
  transfers between devices with their start and end apart: 8 -> 8, of which waited for: 6 -> 3; matrix products, arithmetic and copies ran while one was open for 0% -> 0% of each run, Pallas kernels for 14% -> 25%
where the time goes in v1:
time: 37.9 us; the launch traced here: 38.2 us
  starting transfers between devices  14.9 us (39%)
  Pallas kernels  14.5 us (38%)
  waiting for transfers between devices  7.65 us (20%)
  between operations  0.93 us (2%)
    ppermute x6, starting transfers between devices, around(): arrived.append(lax.ppermute(value, 'gy', pairs) if s and pairs else value)  11.3 us
    pallas_call x2, Pallas kernels, load(): pl.pallas_call(functools.partial(load_kernel, start, stop), name='load',...  6.79 us
    ppermute x6, waiting for transfers between devices, around(): arrived.append(lax.ppermute(value, 'gy', pairs) if s and pairs else value)  5.34 us
    ppermute x2, starting transfers between devices, exchange(): return lax.ppermute(value, BOTH, pairs)  3.61 us
    ppermute x2, waiting for transfers between devices, exchange(): return lax.ppermute(value, BOTH, pairs)  2.31 us
    pallas_call x1, Pallas kernels, relax(): pl.pallas_call(functools.partial(relax_kernel, level), name='relax', out_...  2.17 us
    pallas_call x1, Pallas kernels, multiply(): pl.pallas_call(functools.partial(kernel, group), name=kernel.__name__, ou...  2.11 us
    pallas_call x1, Pallas kernels, prepare(): pl.pallas_call(prepare_kernel, name='prepare', out_shape=(half, half), in...  1.74 us
  transfers between devices with their start and end apart: 8, of which 3 were waited for; matrix products, arithmetic and copies ran while one was open for 0% of the time, Pallas kernels for 25%

profile of v1, /device:TPU:4, one launch (start us, length us, event | category | flops | bytes accessed | tf_op | source)
XLA Modules:
  0.0 38.2 jit_solution(10875097352373180100)
XLA Ops:
  0.0 1.7 %prepare.1 = (bf16[32,8,512]{2,1,0:T(8,128)(2,1)S(1)}, bf16[32,8,512]{2,1,0:T(8,128)(2,1)S(1)}) custom-call(s32[8]{0:T(128)} %level_ref.5, s32[2,64]{1,0:T(2,128)} %link_ref.3, f32[8,32768]{1,0:T(8,128)} %bitcast.8), custom_call_target="tpu_custom_call" | custom-call | flops 1000000 | bytes 2000000 | tf_op jit(solution)/shard_map/prepare/pallas_call | solution.py:111
  1.8 0.1 collective-permute-start.32
  1.8 0.0 copy-start
  1.8 0.0 copy-start.1
  1.9 0.0 copy-start.2
  1.9 0.0 copy-start.3
  1.9 3.5 %collective-permute-start.33 = (bf16[32,8,512]{2,1,0:T(8,128)(2,1)S(1)}, bf16[32,8,512]{2,1,0:T(8,128)(2,1)S(1)}, u32[]{:S(2)}, u32[]{:S(2)}) collective-permute-start(bf16[32,8,512]{2,1,0:T(8,128)(2,1)S(1)} %get-tuple-element.249), channel_id=1, source_target_pairs={{4,8},{8,4},{5,9},{9,5},{6,10},{10,6},{7,11},{11,7},{12,16},{16,12... | collective-permute-start | bytes 786440 | tf_op jit(solution)/shard_map/ppermute | solution.py:672
  5.4 3.5 %load.11 = (s32[1]{0:T(128)}, bf16[8,512,512]{2,1,0:T(8,128)(2,1)S(1)}) custom-call(s32[8]{0:T(128)} %level_ref.5, s32[2,64]{1,0:T(2,128)} %link_ref.3, bf16[2,16,512,512]{3,2,1,0:T(8,128)(2,1)} %values_ref.1), custom_call_target="tpu_custom_call" | custom-call | bytes 4194304 | tf_op jit(solution)/shard_map/load/pallas_call | solution.py:543
  9.6 0.0 copy-done
  9.6 0.0 copy-done.1
  9.6 0.6 %edge_rows.1 = (bf16[32,512]{1,0:T(8,128)(2,1)S(1)}, bf16[32,512]{1,0:T(8,128)(2,1)S(1)}) custom-call(s32[8]{0:T(128)S(1)} %copy-done.1, f32[8,32768]{1,0:T(8,128)S(1)} %bitcast.9), custom_call_target="tpu_custom_call" | custom-call | flops 1000000 | bytes 2000000 | tf_op jit(solution)/shard_map/edge_rows/pallas_call | solution.py:148
  10.2 0.0 collective-permute-done.32
  10.2 2.3 %collective-permute-done.33 = bf16[32,8,512]{2,1,0:T(8,128)(2,1)S(1)} collective-permute-done((bf16[32,8,512]{2,1,0:T(8,128)(2,1)S(1)}, bf16[32,8,512]{2,1,0:T(8,128)(2,1)S(1)}, u32[]{:S(2)}, u32[]{:S(2)}) %collective-permute-start.33) | collective-permute-done | bytes 262176 | tf_op jit(solution)/shard_map/ppermute | solution.py:672
  12.5 0.0 copy-done.2
  12.5 0.0 copy-done.3
  12.5 25.6 %conditional.1 = (f32[1,8,32768]{2,1,0:T(8,128)}) conditional(s32[]{:T(128)} %bitcast.6, (bf16[32,512]{1,0:T(8,128)(2,1)S(1)}, bf16[32,512]{1,0:T(8,128)(2,1)S(1)}, s32[8]{0:T(128)S(1)}, f32[1,8]{1,0:T(1,128)S(1)}, f32[8,32768]{1,0:T(8,128)S(1)}, /*index=5*/bf16[32,8,512]{2,1,0:T(8,128)(2,1)S(1)}, ...), branch_computations={%region_0.0_spmd, %region_1.0_spmd, %region_2.0_spmd, %region_3.0_... | conditional | flops 279535456 | bytes 21204600 | solution.py:726
  12.6 1.5 %collective-permute-start.26 = (bf16[12,8,512]{2,1,0:T(8,128)(2,1)S(1)}, bf16[12,8,512]{2,1,0:T(8,128)(2,1)S(1)}, u32[]{:S(2)}, u32[]{:S(2)}) collective-permute-start(bf16[12,8,512]{2,1,0:T(8,128)(2,1)S(1)} %get-tuple-element.225), channel_id=1, source_target_pairs={{1,2},{2,1},{3,0},{5,6},{6,5},{7,4},{9,10},{10,9},{11,8},{13,14},{... | collective-permute-start | bytes 294920 | tf_op jit(solution)/shard_map/cond/branch_5_fun/ppermute | solution.py:685
  14.0 4.0 %collective-permute-start.27 = (bf16[12,8,512]{2,1,0:T(8,128)(2,1)S(1)}, bf16[12,8,512]{2,1,0:T(8,128)(2,1)S(1)}, u32[]{:S(2)}, u32[]{:S(2)}) collective-permute-start(bf16[12,8,512]{2,1,0:T(8,128)(2,1)S(1)} %get-tuple-element.226), channel_id=1, source_target_pairs={{0,1},{1,0},{2,3},{3,2},{4,5},{5,4},{6,7},{7,6},{8,9},{9,8},{10,11... | collective-permute-start | bytes 294920 | tf_op jit(solution)/shard_map/cond/branch_5_fun/ppermute | solution.py:685
  18.0 1.3 %collective-permute-start.28 = (bf16[8,8,512]{2,1,0:T(8,128)(2,1)S(1)}, bf16[8,8,512]{2,1,0:T(8,128)(2,1)S(1)}, u32[]{:S(2)}, u32[]{:S(2)}) collective-permute-start(bf16[8,8,512]{2,1,0:T(8,128)(2,1)S(1)} %get-tuple-element.234), channel_id=1, source_target_pairs={{2,0},{3,1},{6,4},{7,5},{10,8},{11,9},{14,12},{15,13},{18,16},{19,... | collective-permute-start | bytes 196616 | tf_op jit(solution)/shard_map/cond/branch_5_fun/ppermute | solution.py:685
  19.3 3.3 %load.10 = (s32[1]{0:T(128)}, bf16[8,512,512]{2,1,0:T(8,128)(2,1)S(1)}) custom-call(s32[8]{0:T(128)S(1)} %get-tuple-element.218.level_ref, s32[2,64]{1,0:T(2,128)S(1)} %get-tuple-element.229.link_ref, bf16[2,16,512,512]{3,2,1,0:T(8,128)(2,1)} %get-tuple-element.231.values_ref), custom_call_target="tpu_custom_call" | custom-call | bytes 4194304 | tf_op jit(solution)/shard_map/cond/branch_5_fun/load/pallas_call | solution.py:543
  22.6 2.6 %collective-permute-done.28.refs_1_ = bf16[8,8,512]{2,1,0:T(8,128)(2,1)S(1)} collective-permute-done((bf16[8,8,512]{2,1,0:T(8,128)(2,1)S(1)}, bf16[8,8,512]{2,1,0:T(8,128)(2,1)S(1)}, u32[]{:S(2)}, u32[]{:S(2)}) %collective-permute-start.28) | collective-permute-done | bytes 65568 | tf_op jit(solution)/shard_map/cond/branch_5_fun/ppermute | solution.py:685
  25.2 0.0 collective-permute-done.26.refs_0_.refs_2_
  25.2 0.0 collective-permute-done.27.refs_1_.refs_3_
  25.2 2.1 %to_fine_kernel.3 = (bf16[16,8,512]{2,1,0:T(8,128)(2,1)S(1)}, bf16[16,8,512]{2,1,0:T(8,128)(2,1)S(1)}, bf16[16,8,512]{2,1,0:T(8,128)(2,1)S(1)}, bf16[16,8,512]{2,1,0:T(8,128)(2,1)S(1)}) custom-call(s32[8]{0:T(128)S(1)} %get-tuple-element.218.level_ref, s32[2,64]{1,0:T(2,128)S(1)} %get-tuple-element.229.link_ref, ...), custom_call_target="tpu_custom_call" | custom-call | flops 268435456 | bytes 8388608 | tf_op jit(solution)/shard_map/cond/branch_5_fun/to_fine_kernel/pallas_call | solution.py:564
  27.4 1.3 %collective-permute-start.29 = (bf16[16,8,512]{2,1,0:T(8,128)(2,1)S(1)}, bf16[16,8,512]{2,1,0:T(8,128)(2,1)S(1)}, u32[]{:S(2)}, u32[]{:S(2)}) collective-permute-start(bf16[16,8,512]{2,1,0:T(8,128)(2,1)S(1)} %get-tuple-element.236), channel_id=1, source_target_pairs={{0,2},{1,3},{4,6},{5,7},{8,10},{9,11},{12,14},{13,15},{16,18},{17,... | collective-permute-start | bytes 393224 | tf_op jit(solution)/shard_map/cond/branch_5_fun/ppermute | solution.py:685
  28.7 1.3 %collective-permute-start.30 = (bf16[16,8,512]{2,1,0:T(8,128)(2,1)S(1)}, bf16[16,8,512]{2,1,0:T(8,128)(2,1)S(1)}, u32[]{:S(2)}, u32[]{:S(2)}) collective-permute-start(bf16[16,8,512]{2,1,0:T(8,128)(2,1)S(1)} %get-tuple-element.237), channel_id=1, source_target_pairs={{0,3},{1,2},{4,7},{5,6},{8,11},{9,10},{12,15},{13,14},{16,19},{17,... | collective-permute-start | bytes 393224 | tf_op jit(solution)/shard_map/cond/branch_5_fun/ppermute | solution.py:685
  30.0 1.9 %collective-permute-start.31 = (bf16[16,8,512]{2,1,0:T(8,128)(2,1)S(1)}, bf16[16,8,512]{2,1,0:T(8,128)(2,1)S(1)}, u32[]{:S(2)}, u32[]{:S(2)}) collective-permute-start(bf16[16,8,512]{2,1,0:T(8,128)(2,1)S(1)} %get-tuple-element.238), channel_id=1, source_target_pairs={{0,1},{1,0},{4,5},{5,4},{8,9},{9,8},{12,13},{13,12},{16,17},{17,16... | collective-permute-start | bytes 393224 | tf_op jit(solution)/shard_map/cond/branch_5_fun/ppermute | solution.py:685
  31.9 2.2 %relax.11 = (f32[8,32768]{1,0:T(8,128)}, f32[8,16384]{1,0:T(8,128)S(1)}) custom-call(s32[8]{0:T(128)S(1)} %get-tuple-element.218.level_ref, f32[1,8]{1,0:T(1,128)S(1)} %get-tuple-element.219.rate_ref, f32[8,32768]{1,0:T(8,128)S(1)} %get-tuple-element.220.cells_ref, bf16[32,8,512]{2,1,0:T(8,128)(2,1)S(1)} %get-tuple-element.221.even_ref, ...), custom_call_target="tpu_custom_call" | custom-call | flops 10000000 | bytes 4000000 | tf_op jit(solution)/shard_map/cond/branch_5_fun/relax/pallas_call | solution.py:339
  34.1 0.0 collective-permute-done.29.refs_3_
  34.1 0.0 collective-permute-done.30.refs_4_
  34.1 2.7 %collective-permute-done.31.refs_5_ = bf16[16,8,512]{2,1,0:T(8,128)(2,1)S(1)} collective-permute-done((bf16[16,8,512]{2,1,0:T(8,128)(2,1)S(1)}, bf16[16,8,512]{2,1,0:T(8,128)(2,1)S(1)}, u32[]{:S(2)}, u32[]{:S(2)}) %collective-permute-start.31) | collective-permute-done | bytes 131104 | tf_op jit(solution)/shard_map/cond/branch_5_fun/ppermute | solution.py:685
  36.8 1.0 %finish.9 = f32[8,32768]{1,0:T(8,128)} custom-call(f32[8,16384]{1,0:T(8,128)S(1)} %get-tuple-element.227.refs_0_, f32[8,32768]{1,0:T(8,128)} %get-tuple-element.228.refs_1_, bf16[16,8,512]{2,1,0:T(8,128)(2,1)S(1)} %get-tuple-element.235.refs_2_, bf16[16,8,512]{2,1,0:T(8,128)(2,1)S(1)} %collective-permute-done.29.refs_3_, ...), custom_call_target="tpu_custom_call", output_to_operand_aliasing={{}: (1, {})} | custom-call | flops 1000000 | bytes 1000000 | tf_op jit(solution)/shard_map/cond/branch_5_fun/finish/pallas_call | solution.py:647
  (1 shorter events, 0.0 us)
Async XLA Ops:
  1.8 8.4 %collective-permute-start.32 = (bf16[32,8,512]{2,1,0:T(8,128)(2,1)S(1)}, bf16[32,8,512]{2,1,0:T(8,128)(2,1)S(1)}, u32[]{:S(2)}, u32[]{:S(2)}) collective-permute-start(bf16[32,8,512]{2,1,0:T(8,128)(2,1)S(1)} %get-tuple-element.248), channel_id=1, source_target_pairs={{0,4},{4,0},{1,5},{5,1},{2,6},{6,2},{3,7},{7,3},{8,12},{12,8},{9,1... | collective-permute-start | bytes 786440 | tf_op jit(solution)/shard_map/ppermute | solution.py:672
  1.8 7.7 %copy-start = (f32[1,8,32768]{2,1,0:T(8,128)S(1)}, f32[1,8,32768]{2,1,0:T(8,128)}, u32[]{:S(2)}) copy-start(f32[1,8,32768]{2,1,0:T(8,128)} %param.11) | copy-start | bytes 3145732
  1.8 7.7 %copy-start.1 = (s32[8]{0:T(128)S(1)}, s32[8]{0:T(128)}, u32[]{:S(2)}) copy-start(s32[8]{0:T(128)} %level_ref.5) | copy-start | bytes 100
  1.9 10.7 %copy-start.2 = (s32[2,64]{1,0:T(2,128)S(1)}, s32[2,64]{1,0:T(2,128)}, u32[]{:S(2)}) copy-start(s32[2,64]{1,0:T(2,128)} %link_ref.3) | copy-start | bytes 1540
  1.9 10.6 %copy-start.3 = (f32[1,8]{1,0:T(1,128)S(1)}, f32[1,8]{1,0:T(1,128)}, u32[]{:S(2)}) copy-start(f32[1,8]{1,0:T(1,128)} %param.12) | copy-start | bytes 100
  1.9 10.6 %collective-permute-start.33 = (bf16[32,8,512]{2,1,0:T(8,128)(2,1)S(1)}, bf16[32,8,512]{2,1,0:T(8,128)(2,1)S(1)}, u32[]{:S(2)}, u32[]{:S(2)}) collective-permute-start(bf16[32,8,512]{2,1,0:T(8,128)(2,1)S(1)} %get-tuple-element.249), channel_id=1, source_target_pairs={{4,8},{8,4},{5,9},{9,5},{6,10},{10,6},{7,11},{11,7},{12,16},{16,12... | collective-permute-start | bytes 786440 | tf_op jit(solution)/shard_map/ppermute | solution.py:672
  12.6 12.7 %collective-permute-start.26 = (bf16[12,8,512]{2,1,0:T(8,128)(2,1)S(1)}, bf16[12,8,512]{2,1,0:T(8,128)(2,1)S(1)}, u32[]{:S(2)}, u32[]{:S(2)}) collective-permute-start(bf16[12,8,512]{2,1,0:T(8,128)(2,1)S(1)} %get-tuple-element.225), channel_id=1, source_target_pairs={{1,2},{2,1},{3,0},{5,6},{6,5},{7,4},{9,10},{10,9},{11,8},{13,14},{... | collective-permute-start | bytes 294920 | tf_op jit(solution)/shard_map/cond/branch_5_fun/ppermute | solution.py:685
  14.0 11.2 %collective-permute-start.27 = (bf16[12,8,512]{2,1,0:T(8,128)(2,1)S(1)}, bf16[12,8,512]{2,1,0:T(8,128)(2,1)S(1)}, u32[]{:S(2)}, u32[]{:S(2)}) collective-permute-start(bf16[12,8,512]{2,1,0:T(8,128)(2,1)S(1)} %get-tuple-element.226), channel_id=1, source_target_pairs={{0,1},{1,0},{2,3},{3,2},{4,5},{5,4},{6,7},{7,6},{8,9},{9,8},{10,11... | collective-permute-start | bytes 294920 | tf_op jit(solution)/shard_map/cond/branch_5_fun/ppermute | solution.py:685
  18.0 7.2 %collective-permute-start.28 = (bf16[8,8,512]{2,1,0:T(8,128)(2,1)S(1)}, bf16[8,8,512]{2,1,0:T(8,128)(2,1)S(1)}, u32[]{:S(2)}, u32[]{:S(2)}) collective-permute-start(bf16[8,8,512]{2,1,0:T(8,128)(2,1)S(1)} %get-tuple-element.234), channel_id=1, source_target_pairs={{2,0},{3,1},{6,4},{7,5},{10,8},{11,9},{14,12},{15,13},{18,16},{19,... | collective-permute-start | bytes 196616 | tf_op jit(solution)/shard_map/cond/branch_5_fun/ppermute | solution.py:685
  27.4 6.7 %collective-permute-start.29 = (bf16[16,8,512]{2,1,0:T(8,128)(2,1)S(1)}, bf16[16,8,512]{2,1,0:T(8,128)(2,1)S(1)}, u32[]{:S(2)}, u32[]{:S(2)}) collective-permute-start(bf16[16,8,512]{2,1,0:T(8,128)(2,1)S(1)} %get-tuple-element.236), channel_id=1, source_target_pairs={{0,2},{1,3},{4,6},{5,7},{8,10},{9,11},{12,14},{13,15},{16,18},{17,... | collective-permute-start | bytes 393224 | tf_op jit(solution)/shard_map/cond/branch_5_fun/ppermute | solution.py:685
  28.7 5.4 %collective-permute-start.30 = (bf16[16,8,512]{2,1,0:T(8,128)(2,1)S(1)}, bf16[16,8,512]{2,1,0:T(8,128)(2,1)S(1)}, u32[]{:S(2)}, u32[]{:S(2)}) collective-permute-start(bf16[16,8,512]{2,1,0:T(8,128)(2,1)S(1)} %get-tuple-element.237), channel_id=1, source_target_pairs={{0,3},{1,2},{4,7},{5,6},{8,11},{9,10},{12,15},{13,14},{16,19},{17,... | collective-permute-start | bytes 393224 | tf_op jit(solution)/shard_map/cond/branch_5_fun/ppermute | solution.py:685
  30.0 6.9 %collective-permute-start.31 = (bf16[16,8,512]{2,1,0:T(8,128)(2,1)S(1)}, bf16[16,8,512]{2,1,0:T(8,128)(2,1)S(1)}, u32[]{:S(2)}, u32[]{:S(2)}) collective-permute-start(bf16[16,8,512]{2,1,0:T(8,128)(2,1)S(1)} %get-tuple-element.238), channel_id=1, source_target_pairs={{0,1},{1,0},{4,5},{5,4},{8,9},{9,8},{12,13},{13,12},{16,17},{17,16... | collective-permute-start | bytes 393224 | tf_op jit(solution)/shard_map/cond/branch_5_fun/ppermute | solution.py:685
